TPU v7x, 128 devices: a whole 4x4x4 slice. The times are simulated.
128 devices in a mesh: section: 4 (over z_lo, core), dp: 16 (over y, x), tensor: 2 (over z_hi).
Axes of the slice: x: 4, y: 4, z: 4 (z_hi: 2, z_lo: 2; z = z_hi * 2 + z_lo), core: 2. Of those that a mesh axis runs over, the one named last changes fastest.
Arguments:
- grad_hidden: bfloat16 [4, 2048, 16384], P('section', None, ('dp', 'tensor')), may hold values from -6 to 6
- gate_pre: bfloat16 [4, 2048, 16384], P('section', None, ('dp', 'tensor')), may hold values from -6 to 6
- up_pre: bfloat16 [4, 2048, 16384], P('section', None, ('dp', 'tensor')), may hold values from -6 to 6
- w_gate: bfloat16 [4, 16384, 6144], P('section', ('dp', 'tensor')), may hold values from -0.078125 to 0.078125
- w_up: bfloat16 [4, 16384, 6144], P('section', ('dp', 'tensor')), may hold values from -0.078125 to 0.078125
- block_expert: int32 [4, 16], P('section'), may hold values from 0 to 1
Outputs:
- prev_grad: bfloat16 [4, 2048, 6144], P('section', ('dp', 'tensor'))
Inputs may be any that keep to these rules, and one draw needn't show every extreme that they name: block_expert[s, b] is the expert of rows b * 128 to (b + 1) * 128 - 1 of layer s.
All inputs are finite; a program needn't handle non-finite values.
Results may differ from a plain program's by a relative error of at most 0.019.
Values may be sent and summed in bfloat16 or wider, within the bound.
A program may use at most 192 MiB of HBM per device.

v0:
```python
import jax
import jax.numpy as jnp
from jax import lax
from jax.sharding import PartitionSpec as P

F = 8192
BLOCK = 128


def passed_along(x, axis, by):
    size = lax.axis_size(axis)
    return lax.ppermute(x, axis, [(i, (i + by) % size) for i in range(size)])


def swiglu_grads(grad_rows, gate_rows, up_rows):
    gate_f = gate_rows.astype(jnp.float32)
    sig_gate = jax.nn.sigmoid(gate_f)
    grad_f = grad_rows.astype(jnp.float32)
    grad_gate = (
        grad_f * up_rows.astype(jnp.float32) * sig_gate * (1.0 + gate_f * (1.0 - sig_gate))
    ).astype(jnp.bfloat16)
    grad_up = (grad_f * gate_f * sig_gate).astype(jnp.bfloat16)
    return (grad_gate, grad_up)


def per_device(grad_hidden, gate_pre, up_pre, w_gate, w_up, block_expert):
    grad_local = grad_hidden[0]
    gate_local = gate_pre[0]
    up_local = up_pre[0]
    gate_weight = w_gate[0]
    up_weight = w_up[0]
    layout = block_expert[0]
    hidden_dev = gate_weight.shape[0]
    width = gate_weight.shape[1]
    total_rows = grad_local.shape[0]
    block_count = layout.shape[0]
    pair_count = lax.axis_size("tensor")
    rank_count = lax.axis_size("dp")
    device = lax.axis_index("dp") * pair_count + lax.axis_index("tensor")
    my_expert = device * hidden_dev // F
    half_rows = BLOCK // 2

    def product(first, count, row_scale):
        grad_rows = lax.dynamic_slice_in_dim(grad_local, first, count, 0) * row_scale
        gate_rows = lax.dynamic_slice_in_dim(gate_local, first, count, 0)
        up_rows = lax.dynamic_slice_in_dim(up_local, first, count, 0)
        grad_gate, grad_up = swiglu_grads(grad_rows, gate_rows, up_rows)
        return jnp.dot(grad_gate, gate_weight, preferred_element_type=jnp.float32) + jnp.dot(
            grad_up, up_weight, preferred_element_type=jnp.float32
        )

    pieces = total_rows // (rank_count * pair_count) * lax.axis_size(("dp", "tensor")) // half_rows
    firsts = jnp.arange(pieces, dtype=jnp.int32) * half_rows
    match_table = (firsts // BLOCK)[:, None] == jnp.arange(block_count, dtype=jnp.int32)[None, :]
    owners = jnp.sum(jnp.where(match_table, layout[None, :], 0), axis=1)
    unit_scale = jnp.ones((1, 1), jnp.bfloat16)

    def one_piece(item):
        first, owner = item

        def compute(unused):
            return product(first, half_rows, unit_scale)

        def skipped(unused):
            return jnp.zeros((half_rows, width), jnp.float32)

        return lax.cond(owner == my_expert, compute, skipped, 0)

    summed = lax.psum_scatter(
        lax.map(one_piece, (firsts, owners))
        .reshape(total_rows // (rank_count * pair_count) * lax.axis_size(("dp", "tensor")), width)
        .astype(jnp.bfloat16),
        ("dp", "tensor"),
        scatter_dimension=0,
        tiled=True,
    )
    moved = passed_along(summed, "section", -1)
    return moved[None]


def solution(mesh):
    return jax.shard_map(
        per_device,
        mesh=mesh,
        in_specs=(
            P("section", None, ("dp", "tensor")),
            P("section", None, ("dp", "tensor")),
            P("section", None, ("dp", "tensor")),
            P("section", ("dp", "tensor"), None),
            P("section", ("dp", "tensor"), None),
            P("section", None),
        ),
        out_specs=P("section", ("dp", "tensor"), None),
        check_vma=False,
    )
```

profile of v0, /device:TPU:1, one launch (start us, length us, event | category | flops | bytes accessed | tf_op | source)
XLA Modules:
  0.0 623.1 jit_solution(5399074529135224084)
XLA Ops:
  7.3 237.4 %while.11 = (s32[]{:T(128)}, bf16[32,64,6144]{2,1,0:T(8,128)(2,1)}, s32[32]{0:T(128)S(1)}, s32[]{:T(128)}, bf16[2048,512]{1,0:T(8,128)(2,1)}, /*index=5*/bf16[20...) while((s32[]{:T(128)}, bf16[32,64,6144]{2,1,0:T(8,128)(2,1)}, ...), condition=%wide.region_4.5_spmd.clone, body=%wide.region_1.4_spmd.clone.sunk | while | flops 806780928 | bytes 43582608 | solution.py:70
  18.1 9.1 %conditional.3 = (bf16[1,64,6144]{2,1,0:T(8,128)(2,1)S(1)}) conditional(s32[]{:T(128)} %convert_element_type.76, () %tuple.35, (s32[32]{0:T(128)S(1)}, s32[]{:T(128)}, bf16[2048,512]{1,0:T(8,128)(2,1)}, bf16[2048,512]{1,0:T(8,128)(2,1)}, bf16[2048,512]{1,0:T(8,128)(2,1)}, /*index=5*/bf16[512,6144]{1,0:T(8,128)(2,1)}, ...), branch_computations={%region_2.2_spmd, %region_3.3_spmd.clone} | conditional | flops 806780928 | bytes 42008920 | solution.py:67
  29.4 9.1 %conditional.3 = (bf16[1,64,6144]{2,1,0:T(8,128)(2,1)S(1)}) conditional(s32[]{:T(128)} %convert_element_type.76, () %tuple.35, (s32[32]{0:T(128)S(1)}, s32[]{:T(128)}, bf16[2048,512]{1,0:T(8,128)(2,1)}, bf16[2048,512]{1,0:T(8,128)(2,1)}, bf16[2048,512]{1,0:T(8,128)(2,1)}, /*index=5*/bf16[512,6144]{1,0:T(8,128)(2,1)}, ...), branch_computations={%region_2.2_spmd, %region_3.3_spmd.clone} | conditional | flops 806780928 | bytes 42008920 | solution.py:67
  40.8 9.1 %conditional.3 = (bf16[1,64,6144]{2,1,0:T(8,128)(2,1)S(1)}) conditional(s32[]{:T(128)} %convert_element_type.76, () %tuple.35, (s32[32]{0:T(128)S(1)}, s32[]{:T(128)}, bf16[2048,512]{1,0:T(8,128)(2,1)}, bf16[2048,512]{1,0:T(8,128)(2,1)}, bf16[2048,512]{1,0:T(8,128)(2,1)}, /*index=5*/bf16[512,6144]{1,0:T(8,128)(2,1)}, ...), branch_computations={%region_2.2_spmd, %region_3.3_spmd.clone} | conditional | flops 806780928 | bytes 42008920 | solution.py:67
  43.0 4.3 fusion.13
  52.1 9.1 %conditional.3 = (bf16[1,64,6144]{2,1,0:T(8,128)(2,1)S(1)}) conditional(s32[]{:T(128)} %convert_element_type.76, () %tuple.35, (s32[32]{0:T(128)S(1)}, s32[]{:T(128)}, bf16[2048,512]{1,0:T(8,128)(2,1)}, bf16[2048,512]{1,0:T(8,128)(2,1)}, bf16[2048,512]{1,0:T(8,128)(2,1)}, /*index=5*/bf16[512,6144]{1,0:T(8,128)(2,1)}, ...), branch_computations={%region_2.2_spmd, %region_3.3_spmd.clone} | conditional | flops 806780928 | bytes 42008920 | solution.py:67
  68.2 9.1 %conditional.3 = (bf16[1,64,6144]{2,1,0:T(8,128)(2,1)S(1)}) conditional(s32[]{:T(128)} %convert_element_type.76, () %tuple.35, (s32[32]{0:T(128)S(1)}, s32[]{:T(128)}, bf16[2048,512]{1,0:T(8,128)(2,1)}, bf16[2048,512]{1,0:T(8,128)(2,1)}, bf16[2048,512]{1,0:T(8,128)(2,1)}, /*index=5*/bf16[512,6144]{1,0:T(8,128)(2,1)}, ...), branch_computations={%region_2.2_spmd, %region_3.3_spmd.clone} | conditional | flops 806780928 | bytes 42008920 | solution.py:67
  79.6 9.1 %conditional.3 = (bf16[1,64,6144]{2,1,0:T(8,128)(2,1)S(1)}) conditional(s32[]{:T(128)} %convert_element_type.76, () %tuple.35, (s32[32]{0:T(128)S(1)}, s32[]{:T(128)}, bf16[2048,512]{1,0:T(8,128)(2,1)}, bf16[2048,512]{1,0:T(8,128)(2,1)}, bf16[2048,512]{1,0:T(8,128)(2,1)}, /*index=5*/bf16[512,6144]{1,0:T(8,128)(2,1)}, ...), branch_computations={%region_2.2_spmd, %region_3.3_spmd.clone} | conditional | flops 806780928 | bytes 42008920 | solution.py:67
  105.2 9.1 %conditional.3 = (bf16[1,64,6144]{2,1,0:T(8,128)(2,1)S(1)}) conditional(s32[]{:T(128)} %convert_element_type.76, () %tuple.35, (s32[32]{0:T(128)S(1)}, s32[]{:T(128)}, bf16[2048,512]{1,0:T(8,128)(2,1)}, bf16[2048,512]{1,0:T(8,128)(2,1)}, bf16[2048,512]{1,0:T(8,128)(2,1)}, /*index=5*/bf16[512,6144]{1,0:T(8,128)(2,1)}, ...), branch_computations={%region_2.2_spmd, %region_3.3_spmd.clone} | conditional | flops 806780928 | bytes 42008920 | solution.py:67
  116.5 9.1 %conditional.3 = (bf16[1,64,6144]{2,1,0:T(8,128)(2,1)S(1)}) conditional(s32[]{:T(128)} %convert_element_type.76, () %tuple.35, (s32[32]{0:T(128)S(1)}, s32[]{:T(128)}, bf16[2048,512]{1,0:T(8,128)(2,1)}, bf16[2048,512]{1,0:T(8,128)(2,1)}, bf16[2048,512]{1,0:T(8,128)(2,1)}, /*index=5*/bf16[512,6144]{1,0:T(8,128)(2,1)}, ...), branch_computations={%region_2.2_spmd, %region_3.3_spmd.clone} | conditional | flops 806780928 | bytes 42008920 | solution.py:67
  127.9 9.1 %conditional.3 = (bf16[1,64,6144]{2,1,0:T(8,128)(2,1)S(1)}) conditional(s32[]{:T(128)} %convert_element_type.76, () %tuple.35, (s32[32]{0:T(128)S(1)}, s32[]{:T(128)}, bf16[2048,512]{1,0:T(8,128)(2,1)}, bf16[2048,512]{1,0:T(8,128)(2,1)}, bf16[2048,512]{1,0:T(8,128)(2,1)}, /*index=5*/bf16[512,6144]{1,0:T(8,128)(2,1)}, ...), branch_computations={%region_2.2_spmd, %region_3.3_spmd.clone} | conditional | flops 806780928 | bytes 42008920 | solution.py:67
  130.1 4.3 fusion.13
  139.2 9.1 %conditional.3 = (bf16[1,64,6144]{2,1,0:T(8,128)(2,1)S(1)}) conditional(s32[]{:T(128)} %convert_element_type.76, () %tuple.35, (s32[32]{0:T(128)S(1)}, s32[]{:T(128)}, bf16[2048,512]{1,0:T(8,128)(2,1)}, bf16[2048,512]{1,0:T(8,128)(2,1)}, bf16[2048,512]{1,0:T(8,128)(2,1)}, /*index=5*/bf16[512,6144]{1,0:T(8,128)(2,1)}, ...), branch_computations={%region_2.2_spmd, %region_3.3_spmd.clone} | conditional | flops 806780928 | bytes 42008920 | solution.py:67
  150.5 9.1 %conditional.3 = (bf16[1,64,6144]{2,1,0:T(8,128)(2,1)S(1)}) conditional(s32[]{:T(128)} %convert_element_type.76, () %tuple.35, (s32[32]{0:T(128)S(1)}, s32[]{:T(128)}, bf16[2048,512]{1,0:T(8,128)(2,1)}, bf16[2048,512]{1,0:T(8,128)(2,1)}, bf16[2048,512]{1,0:T(8,128)(2,1)}, /*index=5*/bf16[512,6144]{1,0:T(8,128)(2,1)}, ...), branch_computations={%region_2.2_spmd, %region_3.3_spmd.clone} | conditional | flops 806780928 | bytes 42008920 | solution.py:67
  161.9 9.1 %conditional.3 = (bf16[1,64,6144]{2,1,0:T(8,128)(2,1)S(1)}) conditional(s32[]{:T(128)} %convert_element_type.76, () %tuple.35, (s32[32]{0:T(128)S(1)}, s32[]{:T(128)}, bf16[2048,512]{1,0:T(8,128)(2,1)}, bf16[2048,512]{1,0:T(8,128)(2,1)}, bf16[2048,512]{1,0:T(8,128)(2,1)}, /*index=5*/bf16[512,6144]{1,0:T(8,128)(2,1)}, ...), branch_computations={%region_2.2_spmd, %region_3.3_spmd.clone} | conditional | flops 806780928 | bytes 42008920 | solution.py:67
  173.3 9.1 %conditional.3 = (bf16[1,64,6144]{2,1,0:T(8,128)(2,1)S(1)}) conditional(s32[]{:T(128)} %convert_element_type.76, () %tuple.35, (s32[32]{0:T(128)S(1)}, s32[]{:T(128)}, bf16[2048,512]{1,0:T(8,128)(2,1)}, bf16[2048,512]{1,0:T(8,128)(2,1)}, bf16[2048,512]{1,0:T(8,128)(2,1)}, /*index=5*/bf16[512,6144]{1,0:T(8,128)(2,1)}, ...), branch_computations={%region_2.2_spmd, %region_3.3_spmd.clone} | conditional | flops 806780928 | bytes 42008920 | solution.py:67
  184.6 9.1 %conditional.3 = (bf16[1,64,6144]{2,1,0:T(8,128)(2,1)S(1)}) conditional(s32[]{:T(128)} %convert_element_type.76, () %tuple.35, (s32[32]{0:T(128)S(1)}, s32[]{:T(128)}, bf16[2048,512]{1,0:T(8,128)(2,1)}, bf16[2048,512]{1,0:T(8,128)(2,1)}, bf16[2048,512]{1,0:T(8,128)(2,1)}, /*index=5*/bf16[512,6144]{1,0:T(8,128)(2,1)}, ...), branch_computations={%region_2.2_spmd, %region_3.3_spmd.clone} | conditional | flops 806780928 | bytes 42008920 | solution.py:67
  200.7 9.0 %conditional.3 = (bf16[1,64,6144]{2,1,0:T(8,128)(2,1)S(1)}) conditional(s32[]{:T(128)} %convert_element_type.76, () %tuple.35, (s32[32]{0:T(128)S(1)}, s32[]{:T(128)}, bf16[2048,512]{1,0:T(8,128)(2,1)}, bf16[2048,512]{1,0:T(8,128)(2,1)}, bf16[2048,512]{1,0:T(8,128)(2,1)}, /*index=5*/bf16[512,6144]{1,0:T(8,128)(2,1)}, ...), branch_computations={%region_2.2_spmd, %region_3.3_spmd.clone} | conditional | flops 806780928 | bytes 42008920 | solution.py:67
  212.0 9.1 %conditional.3 = (bf16[1,64,6144]{2,1,0:T(8,128)(2,1)S(1)}) conditional(s32[]{:T(128)} %convert_element_type.76, () %tuple.35, (s32[32]{0:T(128)S(1)}, s32[]{:T(128)}, bf16[2048,512]{1,0:T(8,128)(2,1)}, bf16[2048,512]{1,0:T(8,128)(2,1)}, bf16[2048,512]{1,0:T(8,128)(2,1)}, /*index=5*/bf16[512,6144]{1,0:T(8,128)(2,1)}, ...), branch_computations={%region_2.2_spmd, %region_3.3_spmd.clone} | conditional | flops 806780928 | bytes 42008920 | solution.py:67
  223.4 9.0 %conditional.3 = (bf16[1,64,6144]{2,1,0:T(8,128)(2,1)S(1)}) conditional(s32[]{:T(128)} %convert_element_type.76, () %tuple.35, (s32[32]{0:T(128)S(1)}, s32[]{:T(128)}, bf16[2048,512]{1,0:T(8,128)(2,1)}, bf16[2048,512]{1,0:T(8,128)(2,1)}, bf16[2048,512]{1,0:T(8,128)(2,1)}, /*index=5*/bf16[512,6144]{1,0:T(8,128)(2,1)}, ...), branch_computations={%region_2.2_spmd, %region_3.3_spmd.clone} | conditional | flops 806780928 | bytes 42008920 | solution.py:67
  225.6 4.3 fusion.13
  234.7 9.0 %conditional.3 = (bf16[1,64,6144]{2,1,0:T(8,128)(2,1)S(1)}) conditional(s32[]{:T(128)} %convert_element_type.76, () %tuple.35, (s32[32]{0:T(128)S(1)}, s32[]{:T(128)}, bf16[2048,512]{1,0:T(8,128)(2,1)}, bf16[2048,512]{1,0:T(8,128)(2,1)}, bf16[2048,512]{1,0:T(8,128)(2,1)}, /*index=5*/bf16[512,6144]{1,0:T(8,128)(2,1)}, ...), branch_computations={%region_2.2_spmd, %region_3.3_spmd.clone} | conditional | flops 806780928 | bytes 42008920 | solution.py:67
  244.7 357.9 %reduce-scatter.2.cloned.1.call-done = bf16[64,6144]{1,0:T(8,128)(2,1)} async-done(((bf16[2048,6144]{1,0:T(8,128)(2,1)}), bf16[64,6144]{1,0:T(8,128)(2,1)}) %reduce-scatter.2.cloned.1.call-update) | async-done | bytes 786448 | tf_op jit(solution)/shard_map/reduce_scatter | solution.py:69
  605.2 10.2 %collective-permute-done = bf16[64,6144]{1,0:T(8,128)(2,1)S(1)} collective-permute-done((bf16[64,6144]{1,0:T(8,128)(2,1)}, bf16[64,6144]{1,0:T(8,128)(2,1)S(1)}, u32[]{:S(2)}, u32[]{:S(2)}) %collective-permute-start) | collective-permute-done | bytes 786464 | tf_op jit(solution)/shard_map/ppermute | solution.py:12
  (236 shorter events, 177.1 us)
Async XLA Ops:
  6.5 596.1 %reduce-scatter.2.cloned.1.call-start = ((), (), s32[]{:S(2)}) async-start(), calls=%async_computation.1 | async-start | bytes 25952256 | tf_op jit(solution)/shard_map/reduce_scatter | solution.py:69
  20.3 4.7 copy-start
  31.7 4.7 copy-start
  43.0 4.7 copy-start
  54.3 4.7 copy-start
  70.4 4.7 copy-start
  81.8 4.7 copy-start
  107.4 4.7 copy-start
  118.7 4.7 copy-start
  130.1 4.7 copy-start
  141.4 4.7 copy-start
  152.8 4.7 copy-start
  164.1 4.7 copy-start
  175.5 4.7 copy-start
  186.9 4.7 copy-start
  202.9 4.7 copy-start
  214.3 4.7 copy-start
  225.6 4.7 copy-start
  237.0 4.7 copy-start
  602.6 12.7 %collective-permute-start = (bf16[64,6144]{1,0:T(8,128)(2,1)}, bf16[64,6144]{1,0:T(8,128)(2,1)S(1)}, u32[]{:S(2)}, u32[]{:S(2)}) collective-permute-start(bf16[64,6144]{1,0:T(8,128)(2,1)} %reduce-scatter.2.cloned.1.call-done), channel_id=1, source_target_pairs={{0,96},{32,0},{64,32},{96,64},{1,97},{33,1},{65,33},{97,65},{2,98}... | collective-permute-start | bytes 2359304 | tf_op jit(solution)/shard_map/ppermute | solution.py:12
Sparse Core Ops, SparseCore 0:
  244.8 357.7 reduce-scatter.1
where the time goes:
time: 615 us; the launch traced here: 623 us
  waiting for transfers between devices  368 us (60%)
  matrix products  115 us (19%)
  local copies, waits for them, and re-layouts  70.5 us (11%)
  loops' own time  52.7 us (9%)
  between operations  13.4 us (2%)
    reduce_scatter x1, waiting for transfers between devices, per_device(): lax.psum_scatter(lax.map(one_piece, (firsts, owners)).reshape(total_rows...  358 us
    dot_general x18, matrix products, product(): jnp.dot(grad_gate, gate_weight, preferred_element_type=jnp.float32)  77 us
    dot_general x18, matrix products, product(): jnp.dot(grad_up, up_weight, preferred_element_type=jnp.float32)  38.1 us
    dynamic_slice x50, local copies, waits for them, and re-layouts, per_device(): lax.map(one_piece, (firsts, owners))  30.7 us
    dynamic_update_slice x32, local copies, waits for them, and re-layouts, per_device(): lax.map(one_piece, (firsts, owners))  30.6 us
    another operation x32, loops' own time, one_piece(): return lax.cond(owner == my_expert, compute, skipped, 0)  30.6 us
    another operation x1, loops' own time, per_device(): lax.map(one_piece, (firsts, owners))  22.1 us
  transfers between devices with their start and end apart: 2, of which 2 were waited for; matrix products, arithmetic and copies ran while one was open for 0% of the time, Pallas kernels for 0%

commit v1 on v0

v1 whole, which is shorter than its diff:
```python
import jax
import jax.numpy as jnp
from jax import lax
from jax.experimental import pallas as pl
from jax.experimental.pallas import tpu as pltpu
from jax.sharding import PartitionSpec as P

F = 8192
BLOCK = 128
RING = 4
HALF = BLOCK // 2
CHUNKS = 4
TILE = 256
MESH = pl.DeviceIdType.MESH


def swiglu_grads(grad_rows, gate_rows, up_rows):
    gate_f = gate_rows.astype(jnp.float32)
    sig_gate = jax.nn.sigmoid(gate_f)
    grad_f = grad_rows.astype(jnp.float32)
    grad_gate = grad_f * up_rows.astype(jnp.float32) * sig_gate * (1.0 + gate_f * (1.0 - sig_gate))
    grad_up = grad_f * gate_f * sig_gate
    return grad_gate.astype(jnp.bfloat16), grad_up.astype(jnp.bfloat16)


def kernel(
    acts_hbm, gate_hbm, up_hbm, out_ref,
    acts, weights, first, second, third, near, far, last,
    acts_sem, load_sem, send1, recv1, send2, recv2, send3, recv3, send4, recv4, send5, recv5,
):
    section = lax.axis_index("section")
    dp = lax.axis_index("dp")
    tensor = lax.axis_index("tensor")
    y, x = dp // RING, dp % RING
    hidden = gate_hbm.shape[0]
    width = weights.shape[3]
    part_width = CHUNKS * width

    def turned(value, by):
        return (value + by) % RING

    def at_x(by):
        return (section, y * RING + turned(x, by), tensor)

    def at_y(by):
        return (section, turned(y, by) * RING + x, tensor)

    outer = (x, y)
    inner = (y, x)
    outer_device = (at_x, at_y)
    inner_device = (at_y, at_x)
    before = (section + 3) % 4
    after = (section + 1) % 4

    def load(part, c, kind):
        source = (gate_hbm, up_hbm)[kind]
        columns = pl.ds(pl.multiple_of(part * part_width + c * width, 128), width)
        return pltpu.make_async_copy(
            source.at[:, columns],
            weights.at[part, c, pl.ds(kind * hidden, hidden), :],
            load_sem.at[part, c, kind],
        )

    acts_copy = pltpu.make_async_copy(acts_hbm, acts, acts_sem)
    acts_copy.start()

    @pl.loop(0, CHUNKS)
    def _(c):
        for part in range(2):
            for kind in range(2):
                load(part, c, kind).start()

    barrier = pltpu.get_barrier_semaphore()
    peers = [at_x(1), at_x(3), at_y(1), at_y(3)]
    peers += [(s, dp, t) for s in (before, after) for t in range(2)]
    for peer in peers:
        pl.semaphore_signal(barrier, inc=1, device_id=peer, device_id_type=MESH)
    pl.semaphore_wait(barrier, len(peers))

    def remote(src, dst, send, recv, device):
        return pltpu.make_async_remote_copy(
            src_ref=src, dst_ref=dst, send_sem=send, recv_sem=recv, device_id=device, device_id_type=MESH
        )

    def step1(part, c, way):
        return remote(
            first.at[part, c, way], second.at[part, c, way, way],
            send1.at[part, c, way], recv1.at[part, c, way], outer_device[part](1 if way == 0 else 3),
        )

    def step2(part, c, way):
        return remote(
            second.at[part, c, way], third.at[part, c, way],
            send2.at[part, c, way], recv2.at[part, c, way], outer_device[part](1 if way == 0 else 3),
        )

    def step3(part, c, way):
        return remote(
            third.at[part, c, 0, way, turned(inner[part], 2)], near.at[part, c, way],
            send3.at[part, c, way], recv3.at[part, c, way], inner_device[part](1 if way == 0 else 3),
        )

    def step4(part, c, way):
        by = 1 if way == 0 else 3
        return remote(
            third.at[part, c, 0, :, turned(inner[part], by)], far.at[part, c, way],
            send4.at[part, c, way], recv4.at[part, c, way], inner_device[part](by),
        )

    def step5(part, c, half):
        return remote(
            third.at[part, c, 0, half, inner[part]], last.at[part, c, tensor],
            send5.at[part, c, half], recv5.at[part, c, tensor], (before, dp, half),
        )

    def step5_in(part, c, source):
        return remote(
            third.at[part, c, 0, 0, inner[part]], last.at[part, c, source],
            send5.at[part, c, 0], recv5.at[part, c, source], (before, dp, 0),
        )

    def product(part, c, chunk, j):
        rows = acts[:, chunk] if part == 0 else acts[chunk]
        rows = rows.reshape(RING * BLOCK, 2 * hidden)
        columns = pl.ds(pl.multiple_of(j * TILE, TILE), TILE)
        total = jnp.dot(rows, weights[part, c, :, columns], preferred_element_type=jnp.float32)
        return total.reshape(RING, 2, HALF, TILE), columns

    acts_copy.wait()

    @pl.loop(0, CHUNKS)
    def _(c):
        for part in range(2):
            for kind in range(2):
                load(part, c, kind).wait()

            @pl.loop(0, width // TILE)
            def _(j):
                total, columns = product(part, c, turned(outer[part], 2), j)
                for way in range(2):
                    first[part, c, way, :, :, columns] = total[:, way].astype(jnp.bfloat16)

            for way in range(2):
                step1(part, c, way).start()

    @pl.loop(0, CHUNKS)
    def _(c):
        for part in range(2):
            for way in range(2):
                step1(part, c, way).wait_recv()

                @pl.loop(0, width // TILE)
                def _(j):
                    total, columns = product(part, c, turned(outer[part], 1 if way == 0 else 3), j)
                    held = second[part, c, way, way, :, :, columns].astype(jnp.float32)
                    second[part, c, way, way, :, :, columns] = (total[:, way] + held).astype(jnp.bfloat16)
                    second[part, c, way, 1 - way, :, :, columns] = total[:, 1 - way].astype(jnp.bfloat16)

                step2(part, c, way).start()

    @pl.loop(0, CHUNKS)
    def _(c):
        for part in range(2):
            for way in range(2):
                step2(part, c, way).wait_recv()

            @pl.loop(0, width // TILE)
            def _(j):
                total, columns = product(part, c, outer[part], j)
                for half in range(2):
                    held = third[part, c, 0, half, :, :, columns].astype(jnp.float32)
                    held += third[part, c, 1, half, :, :, columns].astype(jnp.float32)
                    third[part, c, 0, half, :, :, columns] = (total[:, half] + held).astype(jnp.bfloat16)

            for way in range(2):
                step3(part, c, way).start()

    @pl.loop(0, CHUNKS)
    def _(c):
        for part in range(2):
            for way in range(2):
                step3(part, c, way).wait_recv()
                spot = turned(inner[part], 1 if way == 0 else 3)
                total = third[part, c, 0, way, spot].astype(jnp.float32)
                total += near[part, c, way].astype(jnp.float32)
                third[part, c, 0, way, spot] = total.astype(jnp.bfloat16)
                step4(part, c, way).start()

    @pl.loop(0, CHUNKS)
    def _(c):
        for part in range(2):
            for way in range(2):
                step4(part, c, way).wait_recv()
            for half in range(2):
                total = third[part, c, 0, half, inner[part]].astype(jnp.float32)
                total += far[part, c, 0, half].astype(jnp.float32)
                total += far[part, c, 1, half].astype(jnp.float32)
                third[part, c, 0, half, inner[part]] = total.astype(jnp.bfloat16)
                step5(part, c, half).start()

    @pl.loop(0, CHUNKS)
    def _(c):
        for part in range(2):
            for source in range(2):
                step5_in(part, c, source).wait_recv()
            total = last[part, c, 0].astype(jnp.float32) + last[part, c, 1].astype(jnp.float32)
            columns = pl.ds(pl.multiple_of(part * part_width + c * width, 128), width)
            out_ref[:, columns] = total.astype(jnp.bfloat16)

    @pl.loop(0, CHUNKS)
    def _(c):
        for part in range(2):
            for way in range(2):
                for step in (step1, step2, step3, step4, step5):
                    step(part, c, way).wait_send()


def per_device(grad_hidden, gate_pre, up_pre, w_gate, w_up, block_expert):
    hidden, model = w_gate.shape[1:]
    rows = grad_hidden.shape[1]
    width = model // 2 // CHUNKS
    my_expert = (lax.axis_index("dp") * lax.axis_size("tensor") + lax.axis_index("tensor")) * hidden // F
    mine = jnp.repeat(block_expert[0] == my_expert, BLOCK)[:, None]
    pair = swiglu_grads(grad_hidden[0], gate_pre[0], up_pre[0])
    acts = jnp.where(mine, jnp.concatenate(pair, axis=1), jnp.zeros((), jnp.bfloat16))
    acts = acts.reshape(RING, RING, BLOCK, 2 * hidden)
    bf16 = jnp.bfloat16
    dma = pltpu.SemaphoreType.DMA
    out = pl.pallas_call(
        kernel,
        out_shape=jax.ShapeDtypeStruct((HALF, model), bf16),
        in_specs=[pl.BlockSpec(memory_space=pl.ANY)] * 3,
        out_specs=pl.BlockSpec(memory_space=pltpu.VMEM),
        scratch_shapes=[
            pltpu.VMEM((RING, RING, BLOCK, 2 * hidden), bf16),
            pltpu.VMEM((2, CHUNKS, 2 * hidden, width), bf16),
            pltpu.VMEM((2, CHUNKS, 2, RING, HALF, width), bf16),
            pltpu.VMEM((2, CHUNKS, 2, 2, RING, HALF, width), bf16),
            pltpu.VMEM((2, CHUNKS, 2, 2, RING, HALF, width), bf16),
            pltpu.VMEM((2, CHUNKS, 2, HALF, width), bf16),
            pltpu.VMEM((2, CHUNKS, 2, 2, HALF, width), bf16),
            pltpu.VMEM((2, CHUNKS, 2, HALF, width), bf16),
            dma,
            dma((2, CHUNKS, 2)),
        ]
        + [dma((2, CHUNKS, 2))] * 10,
        cost_estimate=pl.CostEstimate(
            flops=4 * rows * hidden * model, bytes_accessed=4 * hidden * (rows + model), transcendentals=0
        ),
        compiler_params=pltpu.CompilerParams(
            collective_id=0, has_side_effects=True, vmem_limit_bytes=60 * 1024 * 1024
        ),
    )(acts, w_gate[0], w_up[0])
    return out[None]


def solution(mesh):
    return jax.shard_map(
        per_device,
        mesh=mesh,
        in_specs=(
            P("section", None, ("dp", "tensor")),
            P("section", None, ("dp", "tensor")),
            P("section", None, ("dp", "tensor")),
            P("section", ("dp", "tensor"), None),
            P("section", ("dp", "tensor"), None),
            P("section", None),
        ),
        out_specs=P("section", ("dp", "tensor"), None),
        check_vma=False,
    )
```

time: 615 us -> 157 us (0.26); the launches traced: 623 us -> 157 us
  waiting for transfers between devices: 368 us -> 0 us
  Pallas kernels: 0 us -> 148 us
  matrix products: 115 us -> 0 us
  local copies, waits for them, and re-layouts: 70.5 us -> 2.15 us
  loops' own time: 52.7 us -> 0 us
  between operations: 13.4 us -> 0.02 us
  other arithmetic: 0.82 us -> 7.3 us
    reduce_scatter x1 -> x0, waiting for transfers between devices: 358 us -> none  [per_device(): lax.psum_scatter(lax.map(one_piece, (firsts, owners)).reshape(total_rows...]
    pallas_call x0 -> x1, Pallas kernels: none -> 148 us  [per_device(): pl.pallas_call(kernel, out_shape=jax.ShapeDtypeStruct((HALF, model), bf16...]
    dot_general x36 -> x0, matrix products: 115 us -> none  [the longest x18 77 us: product(): jnp.dot(grad_gate, gate_weight, preferred_element_type=jnp.float32)]
    another operation x33 -> x0, loops' own time: 52.7 us -> none  [the longest x32 30.6 us: one_piece(): return lax.cond(owner == my_expert, compute, skipped, 0)]
    dynamic_slice x50 -> x0, local copies, waits for them, and re-layouts: 30.7 us -> none  [per_device(): lax.map(one_piece, (firsts, owners))]
    dynamic_update_slice x32 -> x0, local copies, waits for them, and re-layouts: 30.6 us -> none  [per_device(): lax.map(one_piece, (firsts, owners))]
    ppermute x1 -> x0, waiting for transfers between devices: 10.2 us -> none  [passed_along(): return lax.ppermute(x, axis, [(i, (i + by) % size) for i in range(size)])]
    cond x36 -> x0, local copies, waits for them, and re-layouts: 7.35 us -> none
  transfers between devices with their start and end apart: 2 -> 0, of which waited for: 2 -> 0; matrix products, arithmetic and copies ran while one was open for 0% -> 0% of each run, Pallas kernels for 0% -> 0%
where the time goes in v1:
time: 157 us
  Pallas kernels  148 us (94%)
  other arithmetic  7.3 us (5%)
  local copies, waits for them, and re-layouts  2.15 us (1%)
    pallas_call x1, Pallas kernels, per_device(): pl.pallas_call(kernel, out_shape=jax.ShapeDtypeStruct((HALF, model), bf16...  148 us
    convert_element_type x1, other arithmetic, swiglu_grads(): return (grad_gate.astype(jnp.bfloat16), grad_up.astype(jnp.bfloat16))  4.06 us

profile of v1, /device:TPU:1, one launch (start us, length us, event | category | flops | bytes accessed | tf_op | source)
XLA Modules:
  0.0 157.0 jit_solution(9701834393324179230)
XLA Ops:
  0.0 0.7 compare_reduce_fusion
  0.7 0.1 eq.12
  0.8 4.1 %fusion.2 = (bf16[4,4,128,512]{3,2,1,0:T(8,128)(2,1)S(1)}, bf16[4,4,128,512]{3,2,1,0:T(8,128)(2,1)S(1)}) fusion(bf16[4,4,128,512]{3,2,1,0:T(8,128)(2,1)} %bitcast.9, bf16[4,4,128,512]{3,2,1,0:T(8,128)(2,1)} %bitcast.10, bf16[4,4,128,512]{3,2,1,0:T(8,128)(2,1)} %bitcast.11), kind=kLoop, calls=%fused_computation.6 | loop fusion | flops 16777216 | bytes 10485760 | tf_op jit(solution)/shard_map/convert_element_type | solution.py:23
  4.8 2.6 %maximum_select_fusion.acts_hbm = bf16[4,4,128,1024]{3,2,1,0:T(8,128)(2,1)} fusion(bf16[4,4,128,512]{3,2,1,0:T(8,128)(2,1)S(1)} %get-tuple-element.6, bf16[4,4,128,512]{3,2,1,0:T(8,128)(2,1)S(1)} %get-tuple-element.5, pred[4,4]{1,0:T(4,128)(4,1)S(1)} %eq.12), kind=kLoop, calls=%fused_computation.13 | loop fusion | flops 10485760 | bytes 8388624 | tf_op jit(solution)/shard_map/jit(_where)/select_n | solution.py:225
  7.4 147.6 %shard_map.64 = bf16[64,6144]{1,0:T(8,128)(2,1)} custom-call(bf16[4,4,128,1024]{3,2,1,0:T(8,128)(2,1)} %maximum_select_fusion.acts_hbm, bf16[512,6144]{1,0:T(8,128)(2,1)} %bitcast.13, bf16[512,6144]{1,0:T(8,128)(2,1)} %bitcast.14), custom_call_target="tpu_custom_call" | custom-call | flops 25769803776 | bytes 16777216 | tf_op jit(solution)/shard_map/pallas_call | solution.py:229
  155.0 2.1 %copy.8 = bf16[1,64,6144]{2,1,0:T(8,128)(2,1)} copy(bf16[1,64,6144]{2,1,0:T(8,128)(2,1)} %bitcast.12) | data formatting | bytes 1572864

commit v2 on v1

v2 whole, which is shorter than its diff:
```python
import jax
import jax.numpy as jnp
from jax import lax
from jax.experimental import pallas as pl
from jax.experimental.pallas import tpu as pltpu
from jax.sharding import PartitionSpec as P

F = 8192
BLOCK = 128
RING = 4
HALF = BLOCK // 2
QUARTER = HALF // 2
CHUNKS = 5
WIDE = 2
R_CHUNKS = 2
LAGS = (0, 2, 3, 6, 7, 8)
R_LAGS = (0, 3, 5, 6, 11, 12)
TILE = 256
MESH = pl.DeviceIdType.MESH


def swiglu_grads(grad_rows, gate_rows, up_rows, mine):
    gate_f = gate_rows.astype(jnp.float32)
    sig_gate = jax.nn.sigmoid(gate_f)
    grad_f = jnp.where(mine, grad_rows.astype(jnp.float32), 0.0)
    grad_gate = grad_f * up_rows.astype(jnp.float32) * sig_gate * (1.0 + gate_f * (1.0 - sig_gate))
    grad_up = grad_f * gate_f * sig_gate
    return grad_gate.astype(jnp.bfloat16), grad_up.astype(jnp.bfloat16)


def kernel(
    layout_ref, grad_hbm, gate_hbm, up_hbm, w_gate_hbm, w_up_hbm, out_hbm,
    stage, acts, weights,
    first, second, third, across, near, far,
    halved, joined, r_first, r_second, r_third, r_near, r_far,
    stage_sem, load_sem,
    send1, recv1, send2, recv2, send3, recv3, send4, recv4, send5, recv5, send6, recv6,
    r_send0, r_recv0, r_send1, r_recv1, r_send2, r_recv2, r_send4, r_recv4, r_send5, r_recv5, r_send6, r_recv6,
):
    section = lax.axis_index("section")
    dp = lax.axis_index("dp")
    tensor = lax.axis_index("tensor")
    y, x = dp // RING, dp % RING
    hidden = w_gate_hbm.shape[0]
    width = WIDE * TILE
    my_expert = (dp * 2 + tensor) * hidden // F

    def turned(value, by):
        return (value + by) % RING

    def at_x(by):
        return (section, y * RING + turned(x, by), tensor)

    def at_y(by):
        return (section, turned(y, by) * RING + x, tensor)

    outer = (x, y)
    inner = (y, x)
    outer_device = (at_x, at_y)
    inner_device = (at_y, at_x)
    partner = (section, dp, 1 - tensor)
    before = ((section + 3) % 4, dp, tensor)
    after = ((section + 1) % 4, dp, tensor)
    order = (2, 1, 3, 0)

    def fetch(k, kind):
        source = (grad_hbm, gate_hbm, up_hbm)[kind]
        return pltpu.make_async_copy(source.at[:, turned(x, order[k])], stage.at[k % 2, kind], stage_sem.at[k, kind])

    def tile_of(part, c, j):
        return (part * CHUNKS + c) * WIDE + j

    def r_tile_of(part, c):
        return 2 * CHUNKS * WIDE + part * R_CHUNKS + c

    def columns_of(tile, count):
        return pl.ds(pl.multiple_of(tile * TILE, TILE), count * TILE)

    def load(tile, kind):
        source = (w_gate_hbm, w_up_hbm)[kind]
        return pltpu.make_async_copy(
            source.at[:, columns_of(tile, 1)],
            weights.at[tile, pl.ds(kind * hidden, hidden), :],
            load_sem.at[tile, kind],
        )

    def load_start(tile):
        for kind in range(2):
            load(tile, kind).start()

    def load_wait(tile):
        for kind in range(2):
            load(tile, kind).wait()

    for kind in range(3):
        fetch(0, kind).start()
    for j in range(WIDE):
        load_start(tile_of(0, 0, j))
    for kind in range(3):
        fetch(1, kind).start()
    for j in range(WIDE):
        load_start(tile_of(1, 0, j))

    @pl.loop(0, R_CHUNKS)
    def _(c):
        for part in range(2):
            load_start(r_tile_of(part, c))

    @pl.loop(1, CHUNKS)
    def _(c):
        for part in range(2):
            for j in range(WIDE):
                load_start(tile_of(part, c, j))

    barrier = pltpu.get_barrier_semaphore()
    peers = [at_x(1), at_x(3), at_y(1), at_y(3), partner, before, after]
    for peer in peers:
        pl.semaphore_signal(barrier, inc=1, device_id=peer, device_id_type=MESH)

    def make_acts(k):
        for kind in range(3):
            fetch(k, kind).wait()
        column = turned(x, order[k])

        @pl.loop(0, RING)
        def _(row):
            mine = layout_ref[0, row * RING + column] == my_expert
            held = [stage[k % 2, kind, row] for kind in range(3)]
            pair = swiglu_grads(*held, mine)
            acts[row, column, :, :, :hidden] = pair[0]
            acts[row, column, :, :, hidden:] = pair[1]

        if k + 2 < RING:
            for kind in range(3):
                fetch(k + 2, kind).start()

    def remote(src, dst, send, recv, device):
        return pltpu.make_async_remote_copy(
            src_ref=src, dst_ref=dst, send_sem=send, recv_sem=recv, device_id=device, device_id_type=MESH
        )

    def by_way(way):
        return 1 if way == 0 else 3

    def step1(part, c, way):
        return remote(
            first.at[part, c, way], second.at[part, c, way, way],
            send1.at[part, c, way], recv1.at[part, c, way], outer_device[part](by_way(way)),
        )

    def step2(part, c, way):
        return remote(
            second.at[part, c, way], third.at[part, c, way],
            send2.at[part, c, way], recv2.at[part, c, way], outer_device[part](by_way(way)),
        )

    def step3(part, c):
        return remote(
            third.at[part, c, 0, 1 - tensor], across.at[part, c], send3.at[part, c], recv3.at[part, c], partner
        )

    def step4(part, c, way):
        return remote(
            third.at[part, c, 0, tensor, turned(inner[part], 2), pl.ds(way * QUARTER, QUARTER)], near.at[part, c, way],
            send4.at[part, c, way], recv4.at[part, c, way], inner_device[part](by_way(way)),
        )

    def step5(part, c, way):
        return remote(
            third.at[part, c, 0, tensor, turned(inner[part], by_way(way))], far.at[part, c, way],
            send5.at[part, c, way], recv5.at[part, c, way], inner_device[part](by_way(way)),
        )

    def step6(part, c):
        return remote(
            far.at[part, c, 0], out_hbm.at[:, columns_of(tile_of(part, c, 0), WIDE)],
            send6.at[part, c], recv6.at[part, c], before,
        )

    def r_step0(part, c):
        return remote(halved.at[part, c], joined.at[part, c], r_send0.at[part, c], r_recv0.at[part, c], partner)

    def r_step1(part, c, way):
        return remote(
            r_first.at[part, c, pl.ds(2 * way, 2)], r_second.at[part, c, way, pl.ds(2 * way, 2)],
            r_send1.at[part, c, way], r_recv1.at[part, c, way], outer_device[part](by_way(way)),
        )

    def r_step2(part, c, way):
        return remote(
            r_second.at[part, c, way], r_third.at[part, c, way],
            r_send2.at[part, c, way], r_recv2.at[part, c, way], outer_device[part](by_way(way)),
        )

    def r_step4(part, c, way):
        return remote(
            r_third.at[part, c, 0, turned(inner[part], 2), pl.ds(way * QUARTER, QUARTER)], r_near.at[part, c, way],
            r_send4.at[part, c, way], r_recv4.at[part, c, way], inner_device[part](by_way(way)),
        )

    def r_step5(part, c, way):
        return remote(
            r_third.at[part, c, 0, turned(inner[part], by_way(way))], r_far.at[part, c, way],
            r_send5.at[part, c, way], r_recv5.at[part, c, way], inner_device[part](by_way(way)),
        )

    def r_step6(part, c):
        return remote(
            r_far.at[part, c, 0], out_hbm.at[:, columns_of(r_tile_of(part, c), 1)],
            r_send6.at[part, c], r_recv6.at[part, c], before,
        )

    def dot(rows, tile):
        rows = rows.reshape(-1, 2 * hidden)
        return jnp.dot(rows, weights[tile], preferred_element_type=jnp.float32)

    def product(part, c, chunk, j):
        rows = acts[:, chunk] if part == 0 else acts[chunk]
        return dot(rows, tile_of(part, c, j)).reshape(RING, 2, HALF, TILE), columns_of(j, 1)

    def r_product(part, c, chunk):
        rows = acts[:, chunk, tensor] if part == 0 else acts[chunk, :, tensor]
        held = joined[part, c, :, chunk] if part == 0 else joined[part, c, chunk]
        return dot(rows, r_tile_of(part, c)).reshape(RING, HALF, TILE) + held.astype(jnp.float32)

    def phase0(c):
        for part in range(2):
            for j in range(WIDE):
                load_wait(tile_of(part, c, j))

            @pl.loop(0, WIDE)
            def _(j):
                total, columns = product(part, c, turned(outer[part], 2), j)
                for way in range(2):
                    first[part, c, way, :, :, columns] = total[:, way].astype(jnp.bfloat16)

            for way in range(2):
                step1(part, c, way).start()

            if part == 0:

                @pl.when(c == 0)
                def _():
                    for k in range(1, RING):
                        make_acts(k)

    def phase1(c):
        for part in range(2):
            for way in range(2):
                step1(part, c, way).wait_recv()

                @pl.loop(0, WIDE)
                def _(j):
                    total, columns = product(part, c, turned(outer[part], by_way(way)), j)
                    held = second[part, c, way, way, :, :, columns].astype(jnp.float32)
                    second[part, c, way, way, :, :, columns] = (total[:, way] + held).astype(jnp.bfloat16)
                    second[part, c, way, 1 - way, :, :, columns] = total[:, 1 - way].astype(jnp.bfloat16)

                step2(part, c, way).start()

    def phase2(c):
        for part in range(2):
            for way in range(2):
                step2(part, c, way).wait_recv()

            @pl.loop(0, WIDE)
            def _(j):
                total, columns = product(part, c, outer[part], j)
                for half in range(2):
                    held = third[part, c, 0, half, :, :, columns].astype(jnp.float32)
                    held += third[part, c, 1, half, :, :, columns].astype(jnp.float32)
                    third[part, c, 0, half, :, :, columns] = (total[:, half] + held).astype(jnp.bfloat16)

            step3(part, c).start()

    def phase3(c):
        for part in range(2):
            step3(part, c).wait_recv()
            total = third[part, c, 0, tensor].astype(jnp.float32) + across[part, c].astype(jnp.float32)
            third[part, c, 0, tensor] = total.astype(jnp.bfloat16)
            for way in range(2):
                step4(part, c, way).start()

    def phase4(c):
        for part in range(2):
            for way in range(2):
                step4(part, c, way).wait_recv()
                spot = turned(inner[part], by_way(way))
                rows = pl.ds(way * QUARTER, QUARTER)
                total = third[part, c, 0, tensor, spot, rows].astype(jnp.float32)
                total += near[part, c, way].astype(jnp.float32)
                third[part, c, 0, tensor, spot, rows] = total.astype(jnp.bfloat16)
                step5(part, c, way).start()

    def phase5(c):
        for part in range(2):
            for way in range(2):
                step5(part, c, way).wait_recv()
            total = third[part, c, 0, tensor, inner[part]].astype(jnp.float32)
            total += far[part, c, 0].astype(jnp.float32)
            total += far[part, c, 1].astype(jnp.float32)
            far[part, c, 0] = total.astype(jnp.bfloat16)
            step6(part, c).start()

    def r_phase0(c):
        for part in range(2):
            load_wait(r_tile_of(part, c))
            total = dot(acts[:, :, 1 - tensor], r_tile_of(part, c))
            halved[part, c] = total.astype(jnp.bfloat16).reshape(RING, RING, HALF, TILE)
            r_step0(part, c).start()

    def r_phase1(c):
        for part in range(2):
            r_step0(part, c).wait_recv()
            r_first[part, c] = r_product(part, c, turned(outer[part], 2)).astype(jnp.bfloat16)
            for way in range(2):
                r_step1(part, c, way).start()

    def r_phase2(c):
        for part in range(2):
            for way in range(2):
                r_step1(part, c, way).wait_recv()
                total = r_product(part, c, turned(outer[part], by_way(way)))
                here, there = 2 * way, 2 * (1 - way)
                held = r_second[part, c, way, here : here + 2].astype(jnp.float32)
                r_second[part, c, way, here : here + 2] = (total[here : here + 2] + held).astype(jnp.bfloat16)
                r_second[part, c, way, there : there + 2] = total[there : there + 2].astype(jnp.bfloat16)
                r_step2(part, c, way).start()

    def r_phase3(c):
        for part in range(2):
            for way in range(2):
                r_step2(part, c, way).wait_recv()
            total = r_product(part, c, outer[part])
            total += r_third[part, c, 0].astype(jnp.float32)
            total += r_third[part, c, 1].astype(jnp.float32)
            r_third[part, c, 0] = total.astype(jnp.bfloat16)
            for way in range(2):
                r_step4(part, c, way).start()

    def r_phase4(c):
        for part in range(2):
            for way in range(2):
                r_step4(part, c, way).wait_recv()
                spot = turned(inner[part], by_way(way))
                rows = pl.ds(way * QUARTER, QUARTER)
                total = r_third[part, c, 0, spot, rows].astype(jnp.float32)
                total += r_near[part, c, way].astype(jnp.float32)
                r_third[part, c, 0, spot, rows] = total.astype(jnp.bfloat16)
                r_step5(part, c, way).start()

    def r_phase5(c):
        for part in range(2):
            for way in range(2):
                r_step5(part, c, way).wait_recv()
            total = r_third[part, c, 0, inner[part]].astype(jnp.float32)
            total += r_far[part, c, 0].astype(jnp.float32)
            total += r_far[part, c, 1].astype(jnp.float32)
            r_far[part, c, 0] = total.astype(jnp.bfloat16)
            r_step6(part, c).start()

    make_acts(0)
    pl.semaphore_wait(barrier, len(peers))

    phases = (phase0, phase1, phase2, phase3, phase4, phase5)
    r_phases = (r_phase0, r_phase1, r_phase2, r_phase3, r_phase4, r_phase5)

    @pl.loop(0, max(CHUNKS + LAGS[-1], R_CHUNKS + R_LAGS[-1]))
    def _(slot):
        for i in range(6):

            @pl.when((slot >= LAGS[i]) & (slot < CHUNKS + LAGS[i]))
            def _():
                phases[i](slot - LAGS[i])

            @pl.when((slot >= R_LAGS[i]) & (slot < R_CHUNKS + R_LAGS[i]))
            def _():
                r_phases[i](slot - R_LAGS[i])

    @pl.loop(0, CHUNKS)
    def _(c):
        for part in range(2):
            step6(part, c).wait()
            step3(part, c).wait_send()
            for way in range(2):
                for step in (step1, step2, step4, step5):
                    step(part, c, way).wait_send()

    @pl.loop(0, R_CHUNKS)
    def _(c):
        for part in range(2):
            r_step6(part, c).wait()
            r_step0(part, c).wait_send()
            for way in range(2):
                for step in (r_step1, r_step2, r_step4, r_step5):
                    step(part, c, way).wait_send()


def per_device(grad_hidden, gate_pre, up_pre, w_gate, w_up, block_expert):
    hidden, model = w_gate.shape[1:]
    rows = grad_hidden.shape[1]
    width = WIDE * TILE
    blocked = (RING, RING, 2, HALF, hidden)
    dma = pltpu.SemaphoreType.DMA
    anywhere = pl.BlockSpec(memory_space=pl.ANY)

    def room(*shape):
        return pltpu.VMEM(shape, jnp.bfloat16)

    both, single = dma((2, CHUNKS, 2)), dma((2, CHUNKS))
    r_both, r_single = dma((2, R_CHUNKS, 2)), dma((2, R_CHUNKS))
    out = pl.pallas_call(
        kernel,
        out_shape=jax.ShapeDtypeStruct((HALF, model), jnp.bfloat16),
        in_specs=[pl.BlockSpec(memory_space=pltpu.SMEM)] + [anywhere] * 5,
        out_specs=anywhere,
        scratch_shapes=[
            room(2, 3, RING, 2, HALF, hidden),
            room(RING, RING, 2, HALF, 2 * hidden),
            room(model // TILE, 2 * hidden, TILE),
            room(2, CHUNKS, 2, RING, HALF, width),
            room(2, CHUNKS, 2, 2, RING, HALF, width),
            room(2, CHUNKS, 2, 2, RING, HALF, width),
            room(2, CHUNKS, RING, HALF, width),
            room(2, CHUNKS, 2, QUARTER, width),
            room(2, CHUNKS, 2, HALF, width),
            room(2, R_CHUNKS, RING, RING, HALF, TILE),
            room(2, R_CHUNKS, RING, RING, HALF, TILE),
            room(2, R_CHUNKS, RING, HALF, TILE),
            room(2, R_CHUNKS, 2, RING, HALF, TILE),
            room(2, R_CHUNKS, 2, RING, HALF, TILE),
            room(2, R_CHUNKS, 2, QUARTER, TILE),
            room(2, R_CHUNKS, 2, HALF, TILE),
            dma((RING, 3)),
            dma((model // TILE, 2)),
        ]
        + [both] * 4
        + [single] * 2
        + [both] * 4
        + [single] * 2
        + [r_single] * 2
        + [r_both] * 8
        + [r_single] * 2,
        cost_estimate=pl.CostEstimate(
            flops=4 * rows * hidden * model, bytes_accessed=6 * hidden * rows + 4 * hidden * model, transcendentals=0
        ),
        compiler_params=pltpu.CompilerParams(
            collective_id=0, has_side_effects=True, vmem_limit_bytes=61 * 1024 * 1024
        ),
    )(
        block_expert,
        grad_hidden.reshape(blocked),
        gate_pre.reshape(blocked),
        up_pre.reshape(blocked),
        w_gate[0],
        w_up[0],
    )
    return out[None]


def solution(mesh):
    return jax.shard_map(
        per_device,
        mesh=mesh,
        in_specs=(
            P("section", None, ("dp", "tensor")),
            P("section", None, ("dp", "tensor")),
            P("section", None, ("dp", "tensor")),
            P("section", ("dp", "tensor"), None),
            P("section", ("dp", "tensor"), None),
            P("section", None),
        ),
        out_specs=P("section", ("dp", "tensor"), None),
        check_vma=False,
    )
```

time: 157 us -> 137 us (0.87)
  Pallas kernels: 148 us -> 134 us
  other arithmetic: 7.3 us -> 0 us
    pallas_call x1, Pallas kernels: 148 us -> 134 us  [per_device(): pl.pallas_call(kernel, out_shape=jax.ShapeDtypeStruct((HALF, model), jnp....]
    convert_element_type x1 -> x0, other arithmetic: 4.06 us -> none  [swiglu_grads(): return (grad_gate.astype(jnp.bfloat16), grad_up.astype(jnp.bfloat16))]
    select_n x1 -> x0, other arithmetic: 2.57 us -> none  [per_device(): jnp.where(mine, jnp.concatenate(pair, axis=1), jnp.zeros((), jnp.bfloat16))]
where the time goes in v2:
time: 137 us; the launch traced here: 136 us
  Pallas kernels  134 us (98%)
  local copies, waits for them, and re-layouts  2.06 us (2%)
    pallas_call x1, Pallas kernels, per_device(): pl.pallas_call(kernel, out_shape=jax.ShapeDtypeStruct((HALF, model), jnp....  134 us

profile of v2, /device:TPU:1, one launch (start us, length us, event | category | flops | bytes accessed | tf_op | source)
XLA Modules:
  0.0 136.5 jit_solution(18160327393185549933)
XLA Ops:
  0.0 134.4 %shard_map.64 = bf16[64,6144]{1,0:T(8,128)(2,1)} custom-call(s32[1,16]{1,0:T(1,128)} %layout_ref.1, bf16[4,4,2,64,512]{4,3,2,1,0:T(8,128)(2,1)} %bitcast.9, bf16[4,4,2,64,512]{4,3,2,1,0:T(8,128)(2,1)} %bitcast.10, bf16[4,4,2,64,512]{4,3,2,1,0:T(8,128)(2,1)} %bitcast.11, bf16[512,6144]{1,0:T(8,128)(2,1)} %bitcast.7, bf16[512,6144]{1,0:T(8,128)(2,1)} %bitcast.8), custom_call_target="tpu_custom_call" | custom-call | flops 25769803776 | bytes 18874368 | tf_op jit(solution)/shard_map/pallas_call | solution.py:412
  134.4 2.1 %copy.8 = bf16[1,64,6144]{2,1,0:T(8,128)(2,1)} copy(bf16[1,64,6144]{2,1,0:T(8,128)(2,1)} %bitcast.6) | data formatting | bytes 1572864

commit v3 on v2

--- a/solution.py
+++ b/solution.py
@@ -13,18 +13,21 @@
 CHUNKS = 5
 WIDE = 2
 R_CHUNKS = 2
-LAGS = (0, 2, 3, 6, 7, 8)
-R_LAGS = (0, 3, 5, 6, 11, 12)
+LAGS = (0, 2, 3, 5, 6, 7)
+R_LAGS = (0, 4, 5, 6, 7, 9)
 TILE = 256
+STRIP = 16
+UNROLL = 4
 MESH = pl.DeviceIdType.MESH
 
 
 def swiglu_grads(grad_rows, gate_rows, up_rows, mine):
     gate_f = gate_rows.astype(jnp.float32)
-    sig_gate = jax.nn.sigmoid(gate_f)
+    half_tanh = 0.5 * jnp.tanh(0.5 * gate_f)
     grad_f = jnp.where(mine, grad_rows.astype(jnp.float32), 0.0)
-    grad_gate = grad_f * up_rows.astype(jnp.float32) * sig_gate * (1.0 + gate_f * (1.0 - sig_gate))
-    grad_up = grad_f * gate_f * sig_gate
+    scaled = grad_f * (0.5 + half_tanh)
+    grad_up = scaled * gate_f
+    grad_gate = up_rows.astype(jnp.float32) * (scaled + grad_up * (0.5 - half_tanh))
     return grad_gate.astype(jnp.bfloat16), grad_up.astype(jnp.bfloat16)
 
 
@@ -61,11 +64,10 @@
     partner = (section, dp, 1 - tensor)
     before = ((section + 3) % 4, dp, tensor)
     after = ((section + 1) % 4, dp, tensor)
-    order = (2, 1, 3, 0)
 
     def fetch(k, kind):
         source = (grad_hbm, gate_hbm, up_hbm)[kind]
-        return pltpu.make_async_copy(source.at[:, turned(x, order[k])], stage.at[k % 2, kind], stage_sem.at[k, kind])
+        return pltpu.make_async_copy(source.at[:, turned(x, k)], stage.at[k, kind], stage_sem.at[k, kind])
 
     def tile_of(part, c, j):
         return (part * CHUNKS + c) * WIDE + j
@@ -92,47 +94,47 @@
         for kind in range(2):
             load(tile, kind).wait()
 
-    for kind in range(3):
-        fetch(0, kind).start()
-    for j in range(WIDE):
-        load_start(tile_of(0, 0, j))
-    for kind in range(3):
-        fetch(1, kind).start()
-    for j in range(WIDE):
-        load_start(tile_of(1, 0, j))
-
-    @pl.loop(0, R_CHUNKS)
-    def _(c):
-        for part in range(2):
-            load_start(r_tile_of(part, c))
-
-    @pl.loop(1, CHUNKS)
-    def _(c):
-        for part in range(2):
-            for j in range(WIDE):
-                load_start(tile_of(part, c, j))
-
     barrier = pltpu.get_barrier_semaphore()
     peers = [at_x(1), at_x(3), at_y(1), at_y(3), partner, before, after]
     for peer in peers:
         pl.semaphore_signal(barrier, inc=1, device_id=peer, device_id_type=MESH)
 
-    def make_acts(k):
+    for kind in range(3):
+        fetch(2, kind).start()
+    for j in range(WIDE):
+        load_start(tile_of(0, 0, j))
+    for k in (0, 1, 3):
         for kind in range(3):
-            fetch(k, kind).wait()
-        column = turned(x, order[k])
-
-        @pl.loop(0, RING)
-        def _(row):
-            mine = layout_ref[0, row * RING + column] == my_expert
-            held = [stage[k % 2, kind, row] for kind in range(3)]
-            pair = swiglu_grads(*held, mine)
-            acts[row, column, :, :, :hidden] = pair[0]
-            acts[row, column, :, :, hidden:] = pair[1]
-
-        if k + 2 < RING:
-            for kind in range(3):
-                fetch(k + 2, kind).start()
+            fetch(k, kind).start()
+    for j in range(WIDE):
+        load_start(tile_of(1, 0, j))
+
+    def load_rest():
+        @pl.loop(0, R_CHUNKS)
+        def _(c):
+            for part in range(2):
+                load_start(r_tile_of(part, c))
+
+        @pl.loop(1, CHUNKS)
+        def _(c):
+            for part in range(2):
+                for j in range(WIDE):
+                    load_start(tile_of(part, c, j))
+
+    def make_acts(down, along):
+        row, column = turned(y, down), turned(x, along)
+        mine = layout_ref[0, row * RING + column] == my_expert
+
+        @pl.loop(0, 2 * HALF // STRIP // UNROLL)
+        def _(i):
+            for k in range(UNROLL):
+                strip = i * UNROLL + k
+                half = strip // (HALF // STRIP)
+                rows = pl.ds(pl.multiple_of(strip % (HALF // STRIP) * STRIP, STRIP), STRIP)
+                held = [stage[along, kind, row, half, rows] for kind in range(3)]
+                pair = swiglu_grads(*held, mine)
+                acts[row, column, half, rows, :hidden] = pair[0]
+                acts[row, column, half, rows, hidden:] = pair[1]
 
     def remote(src, dst, send, recv, device):
         return pltpu.make_async_remote_copy(
@@ -241,8 +243,14 @@
 
                 @pl.when(c == 0)
                 def _():
-                    for k in range(1, RING):
-                        make_acts(k)
+                    load_rest()
+                    for k in (0, 1, 3):
+                        for kind in range(3):
+                            fetch(k, kind).wait()
+
+                    @pl.loop(0, 3)
+                    def _(i):
+                        make_acts(2, turned(i, 3))
 
     def phase1(c):
         for part in range(2):
@@ -303,6 +311,12 @@
             step6(part, c).start()
 
     def r_phase0(c):
+        @pl.when(c == 0)
+        def _():
+            @pl.loop(0, 9)
+            def _(i):
+                make_acts(turned(i // 3, 3), turned(i % 3, 3))
+
         for part in range(2):
             load_wait(r_tile_of(part, c))
             total = dot(acts[:, :, 1 - tensor], r_tile_of(part, c))
@@ -359,7 +373,13 @@
             r_far[part, c, 0] = total.astype(jnp.bfloat16)
             r_step6(part, c).start()
 
-    make_acts(0)
+    for kind in range(3):
+        fetch(2, kind).wait()
+
+    @pl.loop(0, RING)
+    def _(i):
+        make_acts(i, 2)
+
     pl.semaphore_wait(barrier, len(peers))
 
     phases = (phase0, phase1, phase2, phase3, phase4, phase5)
@@ -415,7 +435,7 @@
         in_specs=[pl.BlockSpec(memory_space=pltpu.SMEM)] + [anywhere] * 5,
         out_specs=anywhere,
         scratch_shapes=[
-            room(2, 3, RING, 2, HALF, hidden),
+            room(RING, 3, RING, 2, HALF, hidden),
             room(RING, RING, 2, HALF, 2 * hidden),
             room(model // TILE, 2 * hidden, TILE),
             room(2, CHUNKS, 2, RING, HALF, width),

time: 137 us -> 133 us (0.971)
  Pallas kernels: 134 us -> 131 us
    pallas_call x1, Pallas kernels: 134 us -> 131 us  [per_device(): pl.pallas_call(kernel, out_shape=jax.ShapeDtypeStruct((HALF, model), jnp....]
where the time goes in v3:
time: 133 us
  Pallas kernels  131 us (98%)
  local copies, waits for them, and re-layouts  2.06 us (2%)
    pallas_call x1, Pallas kernels, per_device(): pl.pallas_call(kernel, out_shape=jax.ShapeDtypeStruct((HALF, model), jnp....  131 us

profile of v3, /device:TPU:1, one launch (start us, length us, event | category | flops | bytes accessed | tf_op | source)
XLA Modules:
  0.0 132.8 jit_solution(10788814024142004420)
XLA Ops:
  0.0 130.7 %shard_map.64 = bf16[64,6144]{1,0:T(8,128)(2,1)} custom-call(s32[1,16]{1,0:T(1,128)} %layout_ref.1, bf16[4,4,2,64,512]{4,3,2,1,0:T(8,128)(2,1)} %bitcast.9, bf16[4,4,2,64,512]{4,3,2,1,0:T(8,128)(2,1)} %bitcast.10, bf16[4,4,2,64,512]{4,3,2,1,0:T(8,128)(2,1)} %bitcast.11, bf16[512,6144]{1,0:T(8,128)(2,1)} %bitcast.7, bf16[512,6144]{1,0:T(8,128)(2,1)} %bitcast.8), custom_call_target="tpu_custom_call" | custom-call | flops 25769803776 | bytes 18874368 | tf_op jit(solution)/shard_map/pallas_call | solution.py:432
  130.7 2.1 %copy.8 = bf16[1,64,6144]{2,1,0:T(8,128)(2,1)} copy(bf16[1,64,6144]{2,1,0:T(8,128)(2,1)} %bitcast.6) | data formatting | bytes 1572864

commit v4 on v3

v4 whole, which is shorter than its diff:
```python
import jax
import jax.numpy as jnp
from jax import lax
from jax.experimental import pallas as pl
from jax.experimental.pallas import tpu as pltpu
from jax.sharding import PartitionSpec as P

F = 8192
BLOCK = 128
RING = 4
HALF = BLOCK // 2
QUARTER = HALF // 2
CHUNKS = 5
LAST = CHUNKS - 1
LAGS = (0, 2, 4, 6, 8, 10)
R_LAGS = (0, 6, 8, 10, 12, 17)
A_LAGS = (8, 10, 12)
TILE = 512
STRIP = 16
UNROLL = 4
MESH = pl.DeviceIdType.MESH


def swiglu_grads(grad_rows, gate_rows, up_rows, mine):
    gate_f = gate_rows.astype(jnp.float32)
    half_tanh = 0.5 * jnp.tanh(0.5 * gate_f)
    grad_f = jnp.where(mine, grad_rows.astype(jnp.float32), 0.0)
    scaled = grad_f * (0.5 + half_tanh)
    grad_up = scaled * gate_f
    grad_gate = up_rows.astype(jnp.float32) * (scaled + grad_up * (0.5 - half_tanh))
    return grad_gate.astype(jnp.bfloat16), grad_up.astype(jnp.bfloat16)


def kernel(
    layout_ref, grad_hbm, gate_hbm, up_hbm, w_gate_hbm, w_up_hbm, out_hbm,
    stage, acts, weights,
    first, second, third, across, near, far,
    halved, joined, r_first, r_second, r_third, r_near, r_far, a_near, a_far, a_last,
    stage_sem, load_sem,
    send1, recv1, send2, recv2, send3, recv3, send4, recv4, send5, recv5, send6, recv6,
    r_send0, r_recv0, r_send1, r_recv1, r_send2, r_recv2, r_send4, r_recv4, r_send5, r_recv5, r_send6, r_recv6,
    a_send4, a_recv4, a_send5, a_recv5, a_send6, a_recv6, out_sem,
):
    section = lax.axis_index("section")
    dp = lax.axis_index("dp")
    tensor = lax.axis_index("tensor")
    y, x = dp // RING, dp % RING
    hidden = w_gate_hbm.shape[0]
    my_expert = (dp * 2 + tensor) * hidden // F

    def turned(value, by):
        return (value + by) % RING

    xs = [turned(x, by) for by in range(RING)]
    ys = [turned(y, by) for by in range(RING)]
    x_devices = [(section, y * RING + xs[by], tensor) for by in range(RING)]
    y_devices = [(section, ys[by] * RING + x, tensor) for by in range(RING)]

    outer = (xs, ys)
    inner = (ys, xs)
    outer_device = (x_devices, y_devices)
    inner_device = (y_devices, x_devices)
    partner = (section, dp, 1 - tensor)
    before = ((section + 3) % 4, dp, tensor)

    def fetch(k, kind):
        source = (grad_hbm, gate_hbm, up_hbm)[kind]
        return pltpu.make_async_copy(source.at[:, xs[k]], stage.at[k, kind], stage_sem.at[k, kind])

    def tile_of(part, c):
        return part * CHUNKS + c

    def r_tile_of(part):
        return 2 * CHUNKS + part

    def columns_of(tile):
        return pl.ds(pl.multiple_of(tile * TILE, TILE), TILE)

    def load(tile, kind):
        source = (w_gate_hbm, w_up_hbm)[kind]
        return pltpu.make_async_copy(
            source.at[:, columns_of(tile)],
            weights.at[tile, pl.ds(kind * hidden, hidden), :],
            load_sem.at[tile, kind],
        )

    def load_start(tile):
        for kind in range(2):
            load(tile, kind).start()

    def load_wait(tile):
        for kind in range(2):
            load(tile, kind).wait()

    barrier = pltpu.get_barrier_semaphore()
    peers = [x_devices[1], x_devices[3], y_devices[1], y_devices[3], partner]
    peers += [((section + by) % 4, dp, half) for by in (1, 3) for half in range(2)]
    for peer in peers:
        pl.semaphore_signal(barrier, inc=1, device_id=peer, device_id_type=MESH)

    for kind in range(3):
        fetch(2, kind).start()
    load_start(tile_of(0, 0))
    for k in (0, 1, 3):
        for kind in range(3):
            fetch(k, kind).start()
    load_start(tile_of(1, 0))

    def load_rest():
        for part in range(2):
            load_start(r_tile_of(part))

        @pl.loop(1, CHUNKS)
        def _(c):
            for part in range(2):
                load_start(tile_of(part, c))

    def make_acts(down, along):
        row, column = turned(y, down), turned(x, along)
        mine = layout_ref[0, row * RING + column] == my_expert

        @pl.loop(0, 2 * HALF // STRIP // UNROLL)
        def _(i):
            for k in range(UNROLL):
                strip = i * UNROLL + k
                half = strip // (HALF // STRIP)
                rows = pl.ds(pl.multiple_of(strip % (HALF // STRIP) * STRIP, STRIP), STRIP)
                held = [stage[along, kind, row, half, rows] for kind in range(3)]
                pair = swiglu_grads(*held, mine)
                acts[row, column, half, rows, :hidden] = pair[0]
                acts[row, column, half, rows, hidden:] = pair[1]

    def remote(src, dst, send, recv, device):
        return pltpu.make_async_remote_copy(
            src_ref=src, dst_ref=dst, send_sem=send, recv_sem=recv, device_id=device, device_id_type=MESH
        )

    def by_way(way):
        return 1 if way == 0 else 3

    def step1(part, c, way):
        return remote(
            first.at[part, c, way], second.at[part, c, way, way],
            send1.at[part, c, way], recv1.at[part, c, way], outer_device[part][by_way(way)],
        )

    def step2(part, c, way):
        return remote(
            second.at[part, c, way], third.at[part, c, way],
            send2.at[part, c, way], recv2.at[part, c, way], outer_device[part][by_way(way)],
        )

    def step3(part, c):
        return remote(
            third.at[part, c, 0, 1 - tensor], across.at[part, c], send3.at[part, c], recv3.at[part, c], partner
        )

    def step4(part, c, way):
        return remote(
            third.at[part, c, 0, tensor, inner[part][2], pl.ds(way * QUARTER, QUARTER)], near.at[part, c, way],
            send4.at[part, c, way], recv4.at[part, c, way], inner_device[part][by_way(way)],
        )

    def step5(part, c, way):
        return remote(
            third.at[part, c, 0, tensor, inner[part][by_way(way)]], far.at[part, c, way],
            send5.at[part, c, way], recv5.at[part, c, way], inner_device[part][by_way(way)],
        )

    def step6(part, c):
        return remote(
            far.at[part, c, 0], out_hbm.at[:, columns_of(tile_of(part, c))],
            send6.at[part, c], recv6.at[part, c], before,
        )

    def r_step0(part):
        return remote(halved.at[part], joined.at[part], r_send0.at[part], r_recv0.at[part], partner)

    def r_step1(part, way):
        return remote(
            r_first.at[part, pl.ds(2 * way, 2)], r_second.at[part, way, pl.ds(2 * way, 2)],
            r_send1.at[part, way], r_recv1.at[part, way], outer_device[part][by_way(way)],
        )

    def r_step2(part, way):
        return remote(
            r_second.at[part, way], r_third.at[part, way],
            r_send2.at[part, way], r_recv2.at[part, way], outer_device[part][by_way(way)],
        )

    def r_step4(part, way):
        return remote(
            r_third.at[part, 0, inner[part][2], pl.ds(way * QUARTER, QUARTER)], r_near.at[part, way],
            r_send4.at[part, way], r_recv4.at[part, way], inner_device[part][by_way(way)],
        )

    def r_step5(part, way):
        return remote(
            r_third.at[part, 0, inner[part][by_way(way)]], r_far.at[part, way],
            r_send5.at[part, way], r_recv5.at[part, way], inner_device[part][by_way(way)],
        )

    def r_step6(part):
        return remote(
            r_far.at[part, 0], out_hbm.at[:, columns_of(r_tile_of(part))],
            r_send6.at[part], r_recv6.at[part], before,
        )

    def a_step4(part, way):
        return remote(
            third.at[part, LAST, 0, way, inner[part][2]], a_near.at[part, way],
            a_send4.at[part, way], a_recv4.at[part, way], inner_device[part][by_way(way)],
        )

    def a_step5(part, way):
        return remote(
            third.at[part, LAST, 0, :, inner[part][by_way(way)]], a_far.at[part, way],
            a_send5.at[part, way], a_recv5.at[part, way], inner_device[part][by_way(way)],
        )

    def a_step6(part, half, source):
        return remote(
            third.at[part, LAST, 0, half, inner[part][0]], a_last.at[part, source],
            a_send6.at[part, half], a_recv6.at[part, source], ((section + 3) % 4, dp, half),
        )

    def a_out(part):
        return pltpu.make_async_copy(
            a_last.at[part, 0], out_hbm.at[:, columns_of(tile_of(part, LAST))], out_sem.at[part]
        )

    def dot(rows, tile):
        rows = rows.reshape(-1, 2 * hidden)
        return jnp.dot(rows, weights[tile], preferred_element_type=jnp.float32)

    def product(part, c, chunk):
        rows = acts[:, chunk] if part == 0 else acts[chunk]
        return dot(rows, tile_of(part, c)).reshape(RING, 2, HALF, TILE)

    def r_product(part, chunk):
        rows = acts[:, chunk, tensor] if part == 0 else acts[chunk, :, tensor]
        held = joined[part, :, chunk] if part == 0 else joined[part, chunk]
        return dot(rows, r_tile_of(part)).reshape(RING, HALF, TILE) + held.astype(jnp.float32)

    def phase0(c):
        for part in range(2):
            load_wait(tile_of(part, c))
            total = product(part, c, outer[part][2]).astype(jnp.bfloat16)
            for way in range(2):
                first[part, c, way] = total[:, way]
                step1(part, c, way).start()

            if part == 0:

                @pl.when(c == 0)
                def _():
                    load_rest()
                    for k in (0, 1, 3):
                        for kind in range(3):
                            fetch(k, kind).wait()

                    @pl.loop(0, 3)
                    def _(i):
                        make_acts(2, turned(i, 3))

    def phase1(c):
        for part in range(2):
            for way in range(2):
                step1(part, c, way).wait_recv()
                total = product(part, c, outer[part][by_way(way)])
                held = second[part, c, way, way].astype(jnp.float32)
                second[part, c, way, way] = (total[:, way] + held).astype(jnp.bfloat16)
                second[part, c, way, 1 - way] = total[:, 1 - way].astype(jnp.bfloat16)
                step2(part, c, way).start()

    def phase2(c):
        for part in range(2):
            for way in range(2):
                step2(part, c, way).wait_recv()
            total = product(part, c, outer[part][0])
            for half in range(2):
                held = third[part, c, 0, half].astype(jnp.float32) + third[part, c, 1, half].astype(jnp.float32)
                third[part, c, 0, half] = (total[:, half] + held).astype(jnp.bfloat16)

            @pl.when(c < LAST)
            def _():
                step3(part, c).start()

            @pl.when(c == LAST)
            def _():
                for way in range(2):
                    a_step4(part, way).start()

    def phase3(c):
        for part in range(2):
            step3(part, c).wait_recv()
            total = third[part, c, 0, tensor].astype(jnp.float32) + across[part, c].astype(jnp.float32)
            third[part, c, 0, tensor] = total.astype(jnp.bfloat16)
            for way in range(2):
                step4(part, c, way).start()

    def phase4(c):
        for part in range(2):
            for way in range(2):
                step4(part, c, way).wait_recv()
                spot = inner[part][by_way(way)]
                rows = pl.ds(way * QUARTER, QUARTER)
                total = third[part, c, 0, tensor, spot, rows].astype(jnp.float32)
                total += near[part, c, way].astype(jnp.float32)
                third[part, c, 0, tensor, spot, rows] = total.astype(jnp.bfloat16)
                step5(part, c, way).start()

    def phase5(c):
        for part in range(2):
            for way in range(2):
                step5(part, c, way).wait_recv()
            total = third[part, c, 0, tensor, inner[part][0]].astype(jnp.float32)
            total += far[part, c, 0].astype(jnp.float32)
            total += far[part, c, 1].astype(jnp.float32)
            far[part, c, 0] = total.astype(jnp.bfloat16)
            step6(part, c).start()

    def r_phase0():
        @pl.loop(0, 9)
        def _(i):
            make_acts(turned(i // 3, 3), turned(i % 3, 3))

        for part in range(2):
            load_wait(r_tile_of(part))
            for k in range(2):
                total = dot(acts[2 * k : 2 * k + 2, :, 1 - tensor], r_tile_of(part)).astype(jnp.bfloat16)
                halved[part, 2 * k : 2 * k + 2] = total.reshape(2, RING, HALF, TILE)
            r_step0(part).start()

    def r_phase1():
        for part in range(2):
            r_step0(part).wait_recv()
            r_first[part] = r_product(part, outer[part][2]).astype(jnp.bfloat16)
            for way in range(2):
                r_step1(part, way).start()

    def r_phase2():
        for part in range(2):
            for way in range(2):
                r_step1(part, way).wait_recv()
                total = r_product(part, outer[part][by_way(way)])
                here, there = 2 * way, 2 * (1 - way)
                held = r_second[part, way, here : here + 2].astype(jnp.float32)
                r_second[part, way, here : here + 2] = (total[here : here + 2] + held).astype(jnp.bfloat16)
                r_second[part, way, there : there + 2] = total[there : there + 2].astype(jnp.bfloat16)
                r_step2(part, way).start()

    def r_phase3():
        for part in range(2):
            for way in range(2):
                r_step2(part, way).wait_recv()
            total = r_product(part, outer[part][0])
            total += r_third[part, 0].astype(jnp.float32)
            total += r_third[part, 1].astype(jnp.float32)
            r_third[part, 0] = total.astype(jnp.bfloat16)
            for way in range(2):
                r_step4(part, way).start()

    def r_phase4():
        for part in range(2):
            for way in range(2):
                r_step4(part, way).wait_recv()
                spot = inner[part][by_way(way)]
                rows = pl.ds(way * QUARTER, QUARTER)
                total = r_third[part, 0, spot, rows].astype(jnp.float32)
                total += r_near[part, way].astype(jnp.float32)
                r_third[part, 0, spot, rows] = total.astype(jnp.bfloat16)
                r_step5(part, way).start()

    def r_phase5():
        for part in range(2):
            for way in range(2):
                r_step5(part, way).wait_recv()
            total = r_third[part, 0, inner[part][0]].astype(jnp.float32)
            total += r_far[part, 0].astype(jnp.float32)
            total += r_far[part, 1].astype(jnp.float32)
            r_far[part, 0] = total.astype(jnp.bfloat16)
            r_step6(part).start()

    def a_phase3():
        for part in range(2):
            for way in range(2):
                a_step4(part, way).wait_recv()
                spot = inner[part][by_way(way)]
                total = third[part, LAST, 0, way, spot].astype(jnp.float32) + a_near[part, way].astype(jnp.float32)
                third[part, LAST, 0, way, spot] = total.astype(jnp.bfloat16)
                a_step5(part, way).start()

    def a_phase4():
        for part in range(2):
            for way in range(2):
                a_step5(part, way).wait_recv()
            for half in range(2):
                total = third[part, LAST, 0, half, inner[part][0]].astype(jnp.float32)
                total += a_far[part, 0, half].astype(jnp.float32)
                total += a_far[part, 1, half].astype(jnp.float32)
                third[part, LAST, 0, half, inner[part][0]] = total.astype(jnp.bfloat16)
                a_step6(part, half, tensor).start()

    def a_phase5():
        for part in range(2):
            for source in range(2):
                a_step6(part, 0, source).wait_recv()
            total = a_last[part, 0].astype(jnp.float32) + a_last[part, 1].astype(jnp.float32)
            a_last[part, 0] = total.astype(jnp.bfloat16)
            a_out(part).start()

    for kind in range(3):
        fetch(2, kind).wait()

    @pl.loop(0, RING)
    def _(i):
        make_acts(i, 2)

    pl.semaphore_wait(barrier, len(peers))

    phases = (phase0, phase1, phase2, phase3, phase4, phase5)
    r_phases = (r_phase0, r_phase1, r_phase2, r_phase3, r_phase4, r_phase5)
    a_phases = (a_phase3, a_phase4, a_phase5)

    @pl.loop(0, max(LAST + LAGS[-1], R_LAGS[-1] + 1, A_LAGS[-1] + 1))
    def _(slot):
        for i in range(6):
            count = CHUNKS if i < 3 else LAST

            @pl.when((slot >= LAGS[i]) & (slot < count + LAGS[i]))
            def _():
                phases[i](slot - LAGS[i])

            if i >= 3:
                pl.when(slot == A_LAGS[i - 3])(a_phases[i - 3])

            pl.when(slot == R_LAGS[i])(r_phases[i])

    @pl.loop(0, CHUNKS)
    def _(c):
        for part in range(2):
            for way in range(2):
                for step in (step1, step2):
                    step(part, c, way).wait_send()

    @pl.loop(0, LAST)
    def _(c):
        for part in range(2):
            step6(part, c).wait()
            step3(part, c).wait_send()
            for way in range(2):
                for step in (step4, step5):
                    step(part, c, way).wait_send()

    for part in range(2):
        a_out(part).wait()
        r_step6(part).wait()
        r_step0(part).wait_send()
        for way in range(2):
            for step in (r_step1, r_step2, r_step4, r_step5, a_step4, a_step5):
                step(part, way).wait_send()
            a_step6(part, way, tensor).wait_send()


def per_device(grad_hidden, gate_pre, up_pre, w_gate, w_up, block_expert):
    hidden, model = w_gate.shape[1:]
    rows = grad_hidden.shape[1]
    blocked = (RING, RING, 2, HALF, hidden)
    dma = pltpu.SemaphoreType.DMA
    anywhere = pl.BlockSpec(memory_space=pl.ANY)

    def room(*shape):
        return pltpu.VMEM(shape, jnp.bfloat16)

    both, single = dma((2, CHUNKS, 2)), dma((2, CHUNKS))
    pairs, two = dma((2, 2)), dma((2,))
    out = pl.pallas_call(
        kernel,
        out_shape=jax.ShapeDtypeStruct((HALF, model), jnp.bfloat16),
        in_specs=[pl.BlockSpec(memory_space=pltpu.SMEM)] + [anywhere] * 5,
        out_specs=anywhere,
        scratch_shapes=[
            room(RING, 3, RING, 2, HALF, hidden),
            room(RING, RING, 2, HALF, 2 * hidden),
            room(model // TILE, 2 * hidden, TILE),
            room(2, CHUNKS, 2, RING, HALF, TILE),
            room(2, CHUNKS, 2, 2, RING, HALF, TILE),
            room(2, CHUNKS, 2, 2, RING, HALF, TILE),
            room(2, LAST, RING, HALF, TILE),
            room(2, LAST, 2, QUARTER, TILE),
            room(2, LAST, 2, HALF, TILE),
            room(2, RING, RING, HALF, TILE),
            room(2, RING, RING, HALF, TILE),
            room(2, RING, HALF, TILE),
            room(2, 2, RING, HALF, TILE),
            room(2, 2, RING, HALF, TILE),
            room(2, 2, QUARTER, TILE),
            room(2, 2, HALF, TILE),
            room(2, 2, HALF, TILE),
            room(2, 2, 2, HALF, TILE),
            room(2, 2, HALF, TILE),
            dma((RING, 3)),
            dma((model // TILE, 2)),
        ]
        + [both] * 4
        + [single] * 2
        + [both] * 4
        + [single] * 2
        + [two] * 2
        + [pairs] * 8
        + [two] * 2
        + [pairs] * 6
        + [two],
        cost_estimate=pl.CostEstimate(
            flops=4 * rows * hidden * model, bytes_accessed=6 * hidden * rows + 4 * hidden * model, transcendentals=0
        ),
        compiler_params=pltpu.CompilerParams(
            collective_id=0, has_side_effects=True, vmem_limit_bytes=61 * 1024 * 1024
        ),
    )(
        block_expert,
        grad_hidden.reshape(blocked),
        gate_pre.reshape(blocked),
        up_pre.reshape(blocked),
        w_gate[0],
        w_up[0],
    )
    return out[None]


def solution(mesh):
    return jax.shard_map(
        per_device,
        mesh=mesh,
        in_specs=(
            P("section", None, ("dp", "tensor")),
            P("section", None, ("dp", "tensor")),
            P("section", None, ("dp", "tensor")),
            P("section", ("dp", "tensor"), None),
            P("section", ("dp", "tensor"), None),
            P("section", None),
        ),
        out_specs=P("section", ("dp", "tensor"), None),
        check_vma=False,
    )
```

time: 133 us -> 131 us (0.985)
  Pallas kernels: 131 us -> 128 us
    pallas_call x1, Pallas kernels: 131 us -> 128 us  [per_device(): pl.pallas_call(kernel, out_shape=jax.ShapeDtypeStruct((HALF, model), jnp....]
where the time goes in v4:
time: 131 us; the launch traced here: 130 us
  Pallas kernels  128 us (98%)
  local copies, waits for them, and re-layouts  2.06 us (2%)
    pallas_call x1, Pallas kernels, per_device(): pl.pallas_call(kernel, out_shape=jax.ShapeDtypeStruct((HALF, model), jnp....  128 us

profile of v4, /device:TPU:1, one launch (start us, length us, event | category | flops | bytes accessed | tf_op | source)
XLA Modules:
  0.0 130.5 jit_solution(15733784906972319483)
XLA Ops:
  0.0 128.4 %shard_map.64 = bf16[64,6144]{1,0:T(8,128)(2,1)} custom-call(s32[1,16]{1,0:T(1,128)} %layout_ref.1, bf16[4,4,2,64,512]{4,3,2,1,0:T(8,128)(2,1)} %bitcast.9, bf16[4,4,2,64,512]{4,3,2,1,0:T(8,128)(2,1)} %bitcast.10, bf16[4,4,2,64,512]{4,3,2,1,0:T(8,128)(2,1)} %bitcast.11, bf16[512,6144]{1,0:T(8,128)(2,1)} %bitcast.7, bf16[512,6144]{1,0:T(8,128)(2,1)} %bitcast.8), custom_call_target="tpu_custom_call" | custom-call | flops 25769803776 | bytes 18874368 | tf_op jit(solution)/shard_map/pallas_call | solution.py:478
  128.4 2.1 %copy.8 = bf16[1,64,6144]{2,1,0:T(8,128)(2,1)} copy(bf16[1,64,6144]{2,1,0:T(8,128)(2,1)} %bitcast.6) | data formatting | bytes 1572864

commit v5 on v4

--- a/solution.py
+++ b/solution.py
@@ -12,9 +12,9 @@
 QUARTER = HALF // 2
 CHUNKS = 5
 LAST = CHUNKS - 1
-LAGS = (0, 2, 4, 6, 8, 10)
-R_LAGS = (0, 6, 8, 10, 12, 17)
-A_LAGS = (8, 10, 12)
+LAGS = (0, 1, 3, 5, 7, 9)
+R_LAGS = (0, 5, 7, 9, 11, 14)
+A_LAGS = (7, 9, 14)
 TILE = 512
 STRIP = 16
 UNROLL = 4
@@ -92,24 +92,22 @@
         for kind in range(2):
             load(tile, kind).wait()
 
+    for kind in range(3):
+        fetch(2, kind).start()
+    load_start(tile_of(0, 0))
+
     barrier = pltpu.get_barrier_semaphore()
     peers = [x_devices[1], x_devices[3], y_devices[1], y_devices[3], partner]
     peers += [((section + by) % 4, dp, half) for by in (1, 3) for half in range(2)]
     for peer in peers:
         pl.semaphore_signal(barrier, inc=1, device_id=peer, device_id_type=MESH)
 
-    for kind in range(3):
-        fetch(2, kind).start()
-    load_start(tile_of(0, 0))
     for k in (0, 1, 3):
         for kind in range(3):
             fetch(k, kind).start()
     load_start(tile_of(1, 0))
 
     def load_rest():
-        for part in range(2):
-            load_start(r_tile_of(part))
-
         @pl.loop(1, CHUNKS)
         def _(c):
             for part in range(2):
@@ -254,7 +252,8 @@
 
                 @pl.when(c == 0)
                 def _():
-                    load_rest()
+                    for part in range(2):
+                        load_start(r_tile_of(part))
                     for k in (0, 1, 3):
                         for kind in range(3):
                             fetch(k, kind).wait()
@@ -263,11 +262,13 @@
                     def _(i):
                         make_acts(2, turned(i, 3))
 
+        pl.when(c == 0)(load_rest)
+
     def phase1(c):
         for part in range(2):
             for way in range(2):
+                total = product(part, c, outer[part][by_way(way)])
                 step1(part, c, way).wait_recv()
-                total = product(part, c, outer[part][by_way(way)])
                 held = second[part, c, way, way].astype(jnp.float32)
                 second[part, c, way, way] = (total[:, way] + held).astype(jnp.bfloat16)
                 second[part, c, way, 1 - way] = total[:, 1 - way].astype(jnp.bfloat16)
@@ -275,9 +276,9 @@
 
     def phase2(c):
         for part in range(2):
+            total = product(part, c, outer[part][0])
             for way in range(2):
                 step2(part, c, way).wait_recv()
-            total = product(part, c, outer[part][0])
             for half in range(2):
                 held = third[part, c, 0, half].astype(jnp.float32) + third[part, c, 1, half].astype(jnp.float32)
                 third[part, c, 0, half] = (total[:, half] + held).astype(jnp.bfloat16)
@@ -342,8 +343,8 @@
     def r_phase2():
         for part in range(2):
             for way in range(2):
+                total = r_product(part, outer[part][by_way(way)])
                 r_step1(part, way).wait_recv()
-                total = r_product(part, outer[part][by_way(way)])
                 here, there = 2 * way, 2 * (1 - way)
                 held = r_second[part, way, here : here + 2].astype(jnp.float32)
                 r_second[part, way, here : here + 2] = (total[here : here + 2] + held).astype(jnp.bfloat16)
@@ -352,9 +353,9 @@
 
     def r_phase3():
         for part in range(2):
+            total = r_product(part, outer[part][0])
             for way in range(2):
                 r_step2(part, way).wait_recv()
-            total = r_product(part, outer[part][0])
             total += r_third[part, 0].astype(jnp.float32)
             total += r_third[part, 1].astype(jnp.float32)
             r_third[part, 0] = total.astype(jnp.bfloat16)

time: 131 us -> 130 us (level)
  no operation moved by 1% of the time
where the time goes in v5:
time: 130 us
  Pallas kernels  128 us (98%)
  local copies, waits for them, and re-layouts  2.06 us (2%)
    pallas_call x1, Pallas kernels, per_device(): pl.pallas_call(kernel, out_shape=jax.ShapeDtypeStruct((HALF, model), jnp....  128 us

profile of v5, /device:TPU:1, one launch (start us, length us, event | category | flops | bytes accessed | tf_op | source)
XLA Modules:
  0.0 130.1 jit_solution(8991005804772737010)
XLA Ops:
  0.0 128.1 %shard_map.64 = bf16[64,6144]{1,0:T(8,128)(2,1)} custom-call(s32[1,16]{1,0:T(1,128)} %layout_ref.1, bf16[4,4,2,64,512]{4,3,2,1,0:T(8,128)(2,1)} %bitcast.9, bf16[4,4,2,64,512]{4,3,2,1,0:T(8,128)(2,1)} %bitcast.10, bf16[4,4,2,64,512]{4,3,2,1,0:T(8,128)(2,1)} %bitcast.11, bf16[512,6144]{1,0:T(8,128)(2,1)} %bitcast.7, bf16[512,6144]{1,0:T(8,128)(2,1)} %bitcast.8), custom_call_target="tpu_custom_call" | custom-call | flops 25769803776 | bytes 18874368 | tf_op jit(solution)/shard_map/pallas_call | solution.py:479
  128.1 2.1 %copy.8 = bf16[1,64,6144]{2,1,0:T(8,128)(2,1)} copy(bf16[1,64,6144]{2,1,0:T(8,128)(2,1)} %bitcast.6) | data formatting | bytes 1572864
